TPU v7x, 128 devices: a whole 4x4x4 slice. The times are simulated.
128 devices in a mesh: row: 8 (over z, x_lo), col: 16 (over y, x_hi, core).
Axes of the slice: x: 4 (x_hi: 2, x_lo: 2; x = x_hi * 2 + x_lo), y: 4, z: 4, core: 2. Of those that a mesh axis runs over, the one named last changes fastest.
Arguments:
- tensor_blocks: bfloat16 [8, 384, 6, 128, 128], P('row', 'col'), may hold values from -6 to 6
- block_list: int32 [8, 384, 2], P('row', 'col'), may hold values from 0 to 15, as said below
- occ_green: bfloat16 [2048, 2048], P(('row', 'col')), may hold values from -0.125 to 0.125
- virt_green: bfloat16 [2048, 2048], P(None, ('row', 'col')), may hold values from -0.125 to 0.125
Outputs:
- polarizability: float32 [8, 6, 6], P('row')
Inputs may be any that keep to these rules, and one draw needn't show every extreme that they name: `block_list`: within the 24 blocks of one device the (m, l) pairs are distinct, every atom block occurs as l once or twice and as m once or twice, so at most 2 blocks of one device share an l, and some l is shared by exactly 2.
All inputs are finite; a program needn't handle non-finite values.
Results may differ from a plain program's by a relative error of at most 0.006.
Values may be sent and summed in bfloat16 or wider, within the bound.
No kernel may reach another device: no remote copies, remote signals or barrier semaphores. Data moves between devices by JAX's collectives and lax.ppermute only.
A program may use at most 128 MiB of HBM per device.

v0:
```python
import jax
import jax.numpy as jnp
from jax import lax
from jax.sharding import PartitionSpec as P

CAP = 2


def shards(tensor_blocks, block_list, occ_green, virt_green):
    col_count = lax.axis_size("col")
    blocks = tensor_blocks[0]
    pairs = block_list[0]
    held = blocks.shape[0]
    width = blocks.shape[-1]
    target = pairs[:, 1]
    first_blocks = pairs[:, 0]
    places = jnp.arange(held)
    slot_rank = jnp.sum(
        (target[None, :] == target[:, None]) & (places[None, :] < places[:, None]), axis=1
    )
    select = (target[:, None, None] == jnp.arange(col_count)[None, :, None]) & (
        slot_rank[:, None, None] == jnp.arange(CAP)[None, None, :]
    )
    send_blocks = jnp.einsum(
        "tdk,tpab->dkpab", select.astype(jnp.bfloat16), blocks, preferred_element_type=jnp.float32
    ).astype(jnp.bfloat16)
    send_first = jnp.sum(select.astype(jnp.int32) * (first_blocks + 1)[:, None, None], axis=0) - 1
    recv_blocks, recv_first = (
        lax.all_to_all(send_blocks, "col", split_axis=0, concat_axis=0, tiled=True),
        lax.all_to_all(send_first, "col", split_axis=0, concat_axis=0, tiled=True),
    )
    slot_total = recv_blocks.shape[0] * recv_blocks.shape[1]
    flat_blocks = recv_blocks.reshape(slot_total, recv_blocks.shape[2], width, width)
    placing = (recv_first.reshape(slot_total)[:, None] == jnp.arange(col_count)[None, :]).astype(
        jnp.bfloat16
    )
    dense_parts = jnp.einsum(
        "sm,spab->pmab", placing, flat_blocks, preferred_element_type=jnp.float32
    )
    dense_tensor = dense_parts.astype(jnp.bfloat16).reshape(
        flat_blocks.shape[1], col_count * width, width
    )
    basis_total = dense_tensor.shape[1]
    occ_half = jnp.einsum(
        "nm,pml->pnl",
        lax.all_gather(occ_green, ("row", "col"), axis=0, tiled=True),
        dense_tensor,
        preferred_element_type=jnp.float32,
    ).astype(jnp.bfloat16)
    turned = lax.all_to_all(occ_half, "col", split_axis=1, concat_axis=2, tiled=True)
    both_sides = jnp.einsum(
        "pnl,ls->pns",
        turned,
        lax.all_gather(virt_green, ("row", "col"), axis=1, tiled=True),
        preferred_element_type=jnp.float32,
    ).astype(jnp.bfloat16)
    partial_polar = jnp.einsum(
        "pns,qsn->pq", both_sides, dense_tensor, preferred_element_type=jnp.float32
    )
    polar_total = lax.psum(partial_polar, "col")
    return (polar_total / float(basis_total))[None]


def solution(mesh):
    in_specs = (
        P("row", "col", None, None, None),
        P("row", "col", None),
        P(("row", "col"), None),
        P(None, ("row", "col")),
    )
    out_specs = P("row", None, None)
    return jax.shard_map(shards, mesh=mesh, in_specs=in_specs, out_specs=out_specs, check_vma=False)
```

profile of v0, /device:TPU:0, one launch (start us, length us, event | category | flops | bytes accessed | tf_op | source)
XLA Modules:
  0.0 585.8 jit_solution(11802510145233425043)
XLA Ops:
  6.5 0.0 all-gather.3.cloned.1.call-start
  6.5 0.7 all-gather.3.cloned.1.call-update
  7.3 0.0 all-gather.5.cloned.1.call-start
  7.3 0.7 all-gather.5.cloned.1.call-update
  8.0 0.8 add_bitcast_fusion.1
  8.8 0.2 convert_reduce_fusion
  9.0 0.1 fusion.28
  9.1 0.7 copy.44
  9.8 7.1 %all-to-all-start.1 = ((s32[16,1,2]{2,1,0:T(1,128)}), s32[16,1,2]{2,1,0:T(1,128)S(1)}, u32[]{:S(2)}, u32[]{:S(2)}) async-start(s32[16,1,2]{2,1,0:T(1,128)} %copy.44), calls=%async_computation.1 | async-start | bytes 16384 | tf_op jit(solution)/shard_map/all_to_all | solution.py:30
  16.9 6.1 %fusion.11 = bf16[16,2,6,128,128]{4,0,3,2,1:T(8,128)(2,1)S(1)} fusion(bf16[24,6,128,128]{3,2,1,0:T(8,128)(2,1)} %bitcast.54, pred[24,2]{0,1:T(4,128)(4,1)S(1)} %iota_compare_fusion.3, pred[24,16]{0,1:T(8,128)(4,1)S(1)} %iota_compare_fusion.2), kind=kOutput, calls=%fused_computation.11 | convolution fusion | flops 154141440 | bytes 11010480 | tf_op jit(solution)/shard_map/tdk,tpab->dkpab/dot_general | solution.py:24
  23.0 4.3 copy.43
  27.4 0.0 all-to-all-done.1
  27.4 7.3 %all-to-all-start = ((bf16[16,2,6,128,128]{4,3,2,1,0:T(8,128)(2,1)}), bf16[16,2,6,128,128]{4,3,2,1,0:T(8,128)(2,1)}, u32[]{:S(2)}, u32[]{:S(2)}) async-start(bf16[16,2,6,128,128]{4,3,2,1,0:T(8,128)(2,1)} %copy.43), calls=%async_computation | async-start | bytes 12582912 | tf_op jit(solution)/shard_map/all_to_all | solution.py:29
  34.6 0.5 broadcast.65
  35.2 0.7 reduce.3
  35.8 0.1 eq.73
  35.9 78.0 %all-to-all-done = bf16[16,2,6,128,128]{4,3,2,1,0:T(8,128)(2,1)} async-done(((bf16[16,2,6,128,128]{4,3,2,1,0:T(8,128)(2,1)}), bf16[16,2,6,128,128]{4,3,2,1,0:T(8,128)(2,1)}, u32[]{:S(2)}, u32[]{:S(2)}) %all-to-all-start) | async-done | bytes 6291488 | tf_op jit(solution)/shard_map/all_to_all | solution.py:29
  113.9 6.6 %convert_bitcast_fusion = bf16[6,16,128,128]{3,1,2,0:T(8,128)(2,1)S(1)} fusion(bf16[32,6,128,128]{3,2,1,0:T(8,128)(2,1)} %bitcast.6, s32[32]{0:T(128)S(1)} %eq.73), kind=kOutput, calls=%fused_computation.14 | convolution fusion | flops 102236672 | bytes 9437312 | tf_op jit(solution)/shard_map/sm,spab->pmab/dot_general | solution.py:37
  120.5 0.8 copy.46
  121.3 159.5 %all-gather.3.cloned.1.call-done = bf16[2048,2048]{1,0:T(8,128)(2,1)} async-done(((bf16[16,2048]{1,0:T(8,128)(2,1)}), bf16[2048,2048]{1,0:T(8,128)(2,1)}) %all-gather.3.cloned.1.call-update) | async-done | bytes 8388624 | tf_op jit(solution)/shard_map/all_gather | solution.py:46
  280.8 10.3 %fusion.20 = bf16[6,2048,128]{1,2,0:T(8,128)(2,1)} fusion(bf16[6,2048,128]{2,1,0:T(8,128)(2,1)S(1)} %bitcast.52, bf16[2048,2048]{1,0:T(8,128)(2,1)} %all-gather.3.cloned.1.call-done), kind=kOutput, calls=%fused_computation.15 | convolution fusion | flops 6444023808 | bytes 14680064 | tf_op jit(solution)/shard_map/nm,pml->pnl/dot_general | solution.py:44
  291.2 6.4 %copy.48 = bf16[6,2048,128]{2,0,1:T(8,128)(2,1)} copy(bf16[6,2048,128]{1,2,0:T(8,128)(2,1)} %fusion.20) | data formatting | bytes 6291456 | tf_op jit(solution)/shard_map/convert_element_type | solution.py:49
  297.6 5.4 all-to-all-start.2
  303.0 5.1 copy.53
  308.0 51.2 %all-to-all-done.2 = bf16[6,2048,128]{2,0,1:T(8,128)(2,1)} async-done(((bf16[6,2048,128]{2,0,1:T(8,128)(2,1)}), bf16[6,2048,128]{2,0,1:T(8,128)(2,1)}, u32[]{:S(2)}, u32[]{:S(2)}) %all-to-all-start.2) | async-done | bytes 3145760 | tf_op jit(solution)/shard_map/all_to_all | solution.py:50
  359.3 5.4 copy.50
  364.7 164.0 %all-gather.5.cloned.1.call-done = bf16[2048,2048]{0,1:T(8,128)(2,1)} async-done(((bf16[2048,16]{0,1:T(8,128)(2,1)}), bf16[2048,2048]{0,1:T(8,128)(2,1)}) %all-gather.5.cloned.1.call-update) | async-done | bytes 8388624 | tf_op jit(solution)/shard_map/all_gather | solution.py:54
  528.7 0.0 copy-start
  528.7 9.3 %fusion.17 = bf16[6,128,2048]{2,1,0:T(8,128)(2,1)S(1)} fusion(bf16[6,128,2048]{1,2,0:T(8,128)(2,1)S(1)} %bitcast.55, bf16[2048,2048]{0,1:T(8,128)(2,1)} %all-gather.5.cloned.1.call-done), kind=kOutput, calls=%fused_computation.13 | convolution fusion | flops 6444023808 | bytes 14680064 | tf_op jit(solution)/shard_map/pnl,ls->pns/dot_general | solution.py:51
  538.0 0.0 copy-done
  538.0 5.7 fusion.25
  543.7 34.6 %psum.7 = f32[6,6]{1,0:T(8,128)S(1)} all-reduce(f32[6,6]{1,0:T(8,128)S(1)} %fusion.25), channel_id=1, replica_groups=mesh['row'=8,'col'=16] {'col'}, use_global_device_ids=true, to_apply=%region_2.0 | all-reduce | flops 36 | bytes 288 | tf_op jit(solution)/shard_map/psum | solution.py:60
  578.4 0.6 copy.54
  (4 shorter events, 0.0 us)
Async XLA Ops:
  6.5 274.3 %all-gather.3.cloned.1.call-start = ((), (), s32[]{:S(2)}) async-start(), calls=%async_computation.3 | async-start | bytes 8454144 | tf_op jit(solution)/shard_map/all_gather | solution.py:46
  7.3 521.5 %all-gather.5.cloned.1.call-start = ((), (), s32[]{:S(2)}) async-start(), calls=%async_computation.4 | async-start | bytes 8454144 | tf_op jit(solution)/shard_map/all_gather | solution.py:54
  9.8 17.6 %all-to-all-start.1 = ((s32[16,1,2]{2,1,0:T(1,128)}), s32[16,1,2]{2,1,0:T(1,128)S(1)}, u32[]{:S(2)}, u32[]{:S(2)}) async-start(s32[16,1,2]{2,1,0:T(1,128)} %copy.44), calls=%async_computation.1 | async-start | bytes 16384 | tf_op jit(solution)/shard_map/all_to_all | solution.py:30
  27.4 86.5 %all-to-all-start = ((bf16[16,2,6,128,128]{4,3,2,1,0:T(8,128)(2,1)}), bf16[16,2,6,128,128]{4,3,2,1,0:T(8,128)(2,1)}, u32[]{:S(2)}, u32[]{:S(2)}) async-start(bf16[16,2,6,128,128]{4,3,2,1,0:T(8,128)(2,1)} %copy.43), calls=%async_computation | async-start | bytes 12582912 | tf_op jit(solution)/shard_map/all_to_all | solution.py:29
  297.6 61.7 %all-to-all-start.2 = ((bf16[6,2048,128]{2,0,1:T(8,128)(2,1)}), bf16[6,2048,128]{2,0,1:T(8,128)(2,1)}, u32[]{:S(2)}, u32[]{:S(2)}) async-start(bf16[6,2048,128]{2,0,1:T(8,128)(2,1)} %copy.48), calls=%async_computation.2 | async-start | bytes 8388608 | tf_op jit(solution)/shard_map/all_to_all | solution.py:50
  528.7 9.3 %copy-start = (bf16[6,2048,128]{1,0,2:T(8,128)(2,1)S(1)}, bf16[6,2048,128]{1,0,2:T(8,128)(2,1)}, u32[]{:S(2)}) copy-start(bf16[6,2048,128]{1,0,2:T(8,128)(2,1)} %copy.53) | copy-start | bytes 9437188
Sparse Core Ops, SparseCore 0:
  9.1 271.7 all-gather.2
  282.6 246.1 all-gather.4
where the time goes:
time: 586 us
  waiting for transfers between devices  454 us (77%)
  matrix products  38 us (6%)
  blocking collectives  34.6 us (6%)
  local copies, waits for them, and re-layouts  23.9 us (4%)
  starting transfers between devices  19.8 us (3%)
  between operations  13.5 us (2%)
    all_gather x1, waiting for transfers between devices, shards(): lax.all_gather(virt_green, ('row', 'col'), axis=1, tiled=True)  164 us
    all_gather x1, waiting for transfers between devices, shards(): lax.all_gather(occ_green, ('row', 'col'), axis=0, tiled=True)  160 us
    all_to_all x1, waiting for transfers between devices, shards(): lax.all_to_all(send_blocks, 'col', split_axis=0, concat_axis=0, tiled=True)  78 us
    all_to_all x1, waiting for transfers between devices, shards(): lax.all_to_all(occ_half, 'col', split_axis=1, concat_axis=2, tiled=True)  51.2 us
    psum x1, blocking collectives, shards(): polar_total = lax.psum(partial_polar, 'col')  34.6 us
  transfers between devices with their start and end apart: 5, of which 4 were waited for; matrix products, arithmetic and copies ran while one was open for 8% of the time, Pallas kernels for 0%

commit v1 on v0

--- a/solution.py
+++ b/solution.py
@@ -57,7 +57,7 @@
     partial_polar = jnp.einsum(
         "pns,qsn->pq", both_sides, dense_tensor, preferred_element_type=jnp.float32
     )
-    polar_total = lax.psum(partial_polar, "col")
+    polar_total = jnp.sum(lax.all_gather(partial_polar, "col"), axis=0)
     return (polar_total / float(basis_total))[None]
 
 

time: 586 us -> 575 us (0.981)
  blocking collectives: 34.6 us -> 21.7 us
    psum x1 -> x0, blocking collectives: 34.6 us -> none  [shards(): polar_total = lax.psum(partial_polar, 'col')]
    all_gather x0 -> x1, blocking collectives: none -> 21.7 us  [shards(): polar_total = jnp.sum(lax.all_gather(partial_polar, 'col'), axis=0)]
where the time goes in v1:
time: 575 us; the launch traced here: 573 us
  waiting for transfers between devices  454 us (79%)
  matrix products  38 us (7%)
  local copies, waits for them, and re-layouts  23.9 us (4%)
  blocking collectives  21.7 us (4%)
  starting transfers between devices  19.8 us (3%)
  between operations  13.5 us (2%)
    all_gather x1, waiting for transfers between devices, shards(): lax.all_gather(virt_green, ('row', 'col'), axis=1, tiled=True)  164 us
    all_gather x1, waiting for transfers between devices, shards(): lax.all_gather(occ_green, ('row', 'col'), axis=0, tiled=True)  160 us
    all_to_all x1, waiting for transfers between devices, shards(): lax.all_to_all(send_blocks, 'col', split_axis=0, concat_axis=0, tiled=True)  78 us
    all_to_all x1, waiting for transfers between devices, shards(): lax.all_to_all(occ_half, 'col', split_axis=1, concat_axis=2, tiled=True)  51.2 us
    all_gather x1, blocking collectives, shards(): polar_total = jnp.sum(lax.all_gather(partial_polar, 'col'), axis=0)  21.7 us
  transfers between devices with their start and end apart: 5, of which 4 were waited for; matrix products, arithmetic and copies ran while one was open for 8% of the time, Pallas kernels for 0%

profile of v1, /device:TPU:0, one launch (start us, length us, event | category | flops | bytes accessed | tf_op | source)
XLA Modules:
  0.0 572.8 jit_solution(8799092122873661746)
XLA Ops:
  6.5 0.0 all-gather.5.cloned.1.call-start
  6.5 0.7 all-gather.5.cloned.1.call-update
  7.3 0.0 all-gather.7.cloned.1.call-start
  7.3 0.7 all-gather.7.cloned.1.call-update
  8.0 0.8 add_bitcast_fusion.1
  8.8 0.2 convert_reduce_fusion
  9.0 0.1 fusion.28
  9.1 0.7 copy.44
  9.8 7.1 %all-to-all-start.1 = ((s32[16,1,2]{2,1,0:T(1,128)}), s32[16,1,2]{2,1,0:T(1,128)S(1)}, u32[]{:S(2)}, u32[]{:S(2)}) async-start(s32[16,1,2]{2,1,0:T(1,128)} %copy.44), calls=%async_computation.1 | async-start | bytes 16384 | tf_op jit(solution)/shard_map/all_to_all | solution.py:30
  16.9 6.1 %fusion.11 = bf16[16,2,6,128,128]{4,0,3,2,1:T(8,128)(2,1)S(1)} fusion(bf16[24,6,128,128]{3,2,1,0:T(8,128)(2,1)} %bitcast.55, pred[24,2]{0,1:T(4,128)(4,1)S(1)} %iota_compare_fusion.3, pred[24,16]{0,1:T(8,128)(4,1)S(1)} %iota_compare_fusion.2), kind=kOutput, calls=%fused_computation.11 | convolution fusion | flops 154141440 | bytes 11010480 | tf_op jit(solution)/shard_map/tdk,tpab->dkpab/dot_general | solution.py:24
  23.0 4.3 copy.43
  27.4 0.0 all-to-all-done.1
  27.4 7.3 %all-to-all-start = ((bf16[16,2,6,128,128]{4,3,2,1,0:T(8,128)(2,1)}), bf16[16,2,6,128,128]{4,3,2,1,0:T(8,128)(2,1)}, u32[]{:S(2)}, u32[]{:S(2)}) async-start(bf16[16,2,6,128,128]{4,3,2,1,0:T(8,128)(2,1)} %copy.43), calls=%async_computation | async-start | bytes 12582912 | tf_op jit(solution)/shard_map/all_to_all | solution.py:29
  34.6 0.5 broadcast.74
  35.2 0.7 reduce.4
  35.8 0.1 eq.73
  35.9 78.0 %all-to-all-done = bf16[16,2,6,128,128]{4,3,2,1,0:T(8,128)(2,1)} async-done(((bf16[16,2,6,128,128]{4,3,2,1,0:T(8,128)(2,1)}), bf16[16,2,6,128,128]{4,3,2,1,0:T(8,128)(2,1)}, u32[]{:S(2)}, u32[]{:S(2)}) %all-to-all-start) | async-done | bytes 6291488 | tf_op jit(solution)/shard_map/all_to_all | solution.py:29
  113.9 6.6 %convert_bitcast_fusion = bf16[6,16,128,128]{3,1,2,0:T(8,128)(2,1)S(1)} fusion(bf16[32,6,128,128]{3,2,1,0:T(8,128)(2,1)} %bitcast.6, s32[32]{0:T(128)S(1)} %eq.73), kind=kOutput, calls=%fused_computation.14 | convolution fusion | flops 102236672 | bytes 9437312 | tf_op jit(solution)/shard_map/sm,spab->pmab/dot_general | solution.py:37
  120.5 0.8 copy.46
  121.3 159.5 %all-gather.5.cloned.1.call-done = bf16[2048,2048]{1,0:T(8,128)(2,1)} async-done(((bf16[16,2048]{1,0:T(8,128)(2,1)}), bf16[2048,2048]{1,0:T(8,128)(2,1)}) %all-gather.5.cloned.1.call-update) | async-done | bytes 8388624 | tf_op jit(solution)/shard_map/all_gather | solution.py:46
  280.8 10.3 %fusion.20 = bf16[6,2048,128]{1,2,0:T(8,128)(2,1)} fusion(bf16[6,2048,128]{2,1,0:T(8,128)(2,1)S(1)} %bitcast.53, bf16[2048,2048]{1,0:T(8,128)(2,1)} %all-gather.5.cloned.1.call-done), kind=kOutput, calls=%fused_computation.15 | convolution fusion | flops 6444023808 | bytes 14680064 | tf_op jit(solution)/shard_map/nm,pml->pnl/dot_general | solution.py:44
  291.2 6.4 %copy.48 = bf16[6,2048,128]{2,0,1:T(8,128)(2,1)} copy(bf16[6,2048,128]{1,2,0:T(8,128)(2,1)} %fusion.20) | data formatting | bytes 6291456 | tf_op jit(solution)/shard_map/convert_element_type | solution.py:49
  297.6 5.4 all-to-all-start.2
  303.0 5.1 copy.53
  308.0 51.2 %all-to-all-done.2 = bf16[6,2048,128]{2,0,1:T(8,128)(2,1)} async-done(((bf16[6,2048,128]{2,0,1:T(8,128)(2,1)}), bf16[6,2048,128]{2,0,1:T(8,128)(2,1)}, u32[]{:S(2)}, u32[]{:S(2)}) %all-to-all-start.2) | async-done | bytes 3145760 | tf_op jit(solution)/shard_map/all_to_all | solution.py:50
  359.3 5.4 copy.50
  364.7 164.0 %all-gather.7.cloned.1.call-done = bf16[2048,2048]{0,1:T(8,128)(2,1)} async-done(((bf16[2048,16]{0,1:T(8,128)(2,1)}), bf16[2048,2048]{0,1:T(8,128)(2,1)}) %all-gather.7.cloned.1.call-update) | async-done | bytes 8388624 | tf_op jit(solution)/shard_map/all_gather | solution.py:54
  528.7 0.0 copy-start
  528.7 9.3 %fusion.17 = bf16[6,128,2048]{2,1,0:T(8,128)(2,1)S(1)} fusion(bf16[6,128,2048]{1,2,0:T(8,128)(2,1)S(1)} %bitcast.56, bf16[2048,2048]{0,1:T(8,128)(2,1)} %all-gather.7.cloned.1.call-done), kind=kOutput, calls=%fused_computation.13 | convolution fusion | flops 6444023808 | bytes 14680064 | tf_op jit(solution)/shard_map/pnl,ls->pns/dot_general | solution.py:51
  538.0 0.0 copy-done
  538.0 5.7 fusion.25
  543.7 21.7 %all-gather.1 = f32[16,6,6]{2,1,0:T(8,128)S(1)} all-gather(f32[1,6,6]{2,1,0:T(8,128)S(1)} %fusion.25), channel_id=2, replica_groups=mesh['row'=8,'col'=16] {'col'}, dimensions={0}, use_global_device_ids=true | all-gather | bytes 2448 | tf_op jit(solution)/shard_map/all_gather | solution.py:60
  565.4 0.6 copy.54
  (5 shorter events, 0.1 us)
Async XLA Ops:
  6.5 274.3 %all-gather.5.cloned.1.call-start = ((), (), s32[]{:S(2)}) async-start(), calls=%async_computation.3 | async-start | bytes 8454144 | tf_op jit(solution)/shard_map/all_gather | solution.py:46
  7.3 521.5 %all-gather.7.cloned.1.call-start = ((), (), s32[]{:S(2)}) async-start(), calls=%async_computation.4 | async-start | bytes 8454144 | tf_op jit(solution)/shard_map/all_gather | solution.py:54
  9.8 17.6 %all-to-all-start.1 = ((s32[16,1,2]{2,1,0:T(1,128)}), s32[16,1,2]{2,1,0:T(1,128)S(1)}, u32[]{:S(2)}, u32[]{:S(2)}) async-start(s32[16,1,2]{2,1,0:T(1,128)} %copy.44), calls=%async_computation.1 | async-start | bytes 16384 | tf_op jit(solution)/shard_map/all_to_all | solution.py:30
  27.4 86.5 %all-to-all-start = ((bf16[16,2,6,128,128]{4,3,2,1,0:T(8,128)(2,1)}), bf16[16,2,6,128,128]{4,3,2,1,0:T(8,128)(2,1)}, u32[]{:S(2)}, u32[]{:S(2)}) async-start(bf16[16,2,6,128,128]{4,3,2,1,0:T(8,128)(2,1)} %copy.43), calls=%async_computation | async-start | bytes 12582912 | tf_op jit(solution)/shard_map/all_to_all | solution.py:29
  297.6 61.7 %all-to-all-start.2 = ((bf16[6,2048,128]{2,0,1:T(8,128)(2,1)}), bf16[6,2048,128]{2,0,1:T(8,128)(2,1)}, u32[]{:S(2)}, u32[]{:S(2)}) async-start(bf16[6,2048,128]{2,0,1:T(8,128)(2,1)} %copy.48), calls=%async_computation.2 | async-start | bytes 8388608 | tf_op jit(solution)/shard_map/all_to_all | solution.py:50
  528.7 9.3 %copy-start = (bf16[6,2048,128]{1,0,2:T(8,128)(2,1)S(1)}, bf16[6,2048,128]{1,0,2:T(8,128)(2,1)}, u32[]{:S(2)}) copy-start(bf16[6,2048,128]{1,0,2:T(8,128)(2,1)} %copy.53) | copy-start | bytes 9437188
Sparse Core Ops, SparseCore 0:
  9.1 271.7 all-gather.4
  282.6 246.1 all-gather.6
